TPU v7x, 32 devices: a whole 2x2x4 slice. The times are simulated.
32 devices in a mesh: gx: 8 (over y, x, core), vert: 4 (over z).
Axes of the slice: x: 2, y: 2, z: 4, core: 2. Of those that a mesh axis runs over, the one named last changes fastest.
Arguments:
- distribution: float32 [2, 96, 96, 1024], P(None, 'vert', None, 'gx'), may hold values from 0 to 4, as said below
- wall_type: int32 [2, 64], P(None, 'gx'), may hold values from 0 to 2
- wall_temp_index: int32 [2, 64], P(None, 'gx'), may hold values from 0 to 1
- wall_temps: float32 [2], replicated, may hold values from 0.5 to 2
- accommodation: int32 [3], replicated, may hold values from 0 to 50
Outputs:
- advanced: float32 [2, 96, 96, 1024], P(None, 'vert', None, 'gx')
Inputs may be any that keep to these rules, and one draw needn't show every extreme that they name: `distribution`: nonnegative phase-space densities.
All inputs are finite; a program needn't handle non-finite values.
Results may differ from a plain program's by a relative error of at most 0.0003.
Values sent between devices are 32-bit elements; how exact they have to be, the bound alone decides.
No kernel may reach another device: no remote copies, remote signals or barrier semaphores. Data moves between devices by JAX's collectives and lax.ppermute only.
A program may use at most 128 MiB of HBM per device.

v0:
```python
import math

import jax
import jax.numpy as jnp
from jax import lax
from jax.sharding import PartitionSpec as P

SPEED_NODES_HORIZ = 96
SPEED_NODES_VERT = 96
Y = 16
ITERS = 4
NTEMP = 2
NTYPE = 3


vmax_speed = 4.5
courant = 0.5
diffusivity_ratio = 2.0 / 3.0
relaxation_multiplier = 2.5
shear_exponent = 0.19
time_increment = courant / vmax_speed
highest = lax.Precision.HIGHEST


def with_halo(cells, sides, width):
    for axis, dim in sides:
        count = lax.axis_size(axis)
        head = lax.slice_in_dim(cells, 0, width, axis=dim)
        tail = lax.slice_in_dim(cells, cells.shape[dim] - width, cells.shape[dim], axis=dim)
        cells = jnp.concatenate(
            [
                lax.ppermute(tail, axis, [(i, (i + 1) % count) for i in range(count)]),
                cells,
                lax.ppermute(head, axis, [((i + 1) % count, i) for i in range(count)]),
            ],
            axis=dim,
        )
    return cells


def swapped(value, axis, apart):
    mask = 2**apart
    pairs = [(source, source ^ mask) for source in range(lax.axis_size(axis))]
    return lax.ppermute(value, axis, pairs)


def speeds(number):
    return vmax_speed * (2.0 * jnp.arange(number, dtype=jnp.float32) + 1.0 - number) / number


def band_speeds(vert_index, band_rows):
    offset = jnp.arange(band_rows, dtype=jnp.int32)
    lower = vert_index // 2 * band_rows + offset
    velocity = jnp.where(vert_index % 2 == 0, lower, SPEED_NODES_VERT - 1 - lower)
    return (
        vmax_speed
        * (2.0 * velocity.astype(jnp.float32) + 1.0 - SPEED_NODES_VERT)
        / SPEED_NODES_VERT
    )


def cell_weight():
    return 2.0 * vmax_speed / SPEED_NODES_HORIZ * (2.0 * vmax_speed / SPEED_NODES_VERT)


def shift_flat(values, offset):
    extent = abs(offset)
    padding = jnp.zeros(values.shape[:-1] + (extent,), values.dtype)
    if offset > 0:
        return jnp.concatenate([padding, values[..., :-extent]], axis=-1)
    return jnp.concatenate([values[..., extent:], padding], axis=-1)


def beam_term(center, linear_integral_term, quadratic_integral_term, number):
    return -0.5 * number * (
        3.0 * center - 4.0 * linear_integral_term + quadratic_integral_term
    ) + 0.5 * number * number * (center - 2.0 * linear_integral_term + quadratic_integral_term)


def shakhov_target(speed_x, speed_y, macroscopic_quantities):
    (
        particle_concentration,
        bulk_flow_horizontal,
        bulk_flow_vertical,
        thermal_level,
        thermal_current_horizontal,
        thermal_current_vertical,
    ) = macroscopic_quantities
    relative_speed_horizontal = speed_x[None, :, None] - bulk_flow_horizontal
    relative_speed_vertical = speed_y[:, None, None] - bulk_flow_vertical
    kinetic_content_sum = (
        relative_speed_horizontal * relative_speed_horizontal
        + relative_speed_vertical * relative_speed_vertical
    ) / thermal_level
    relaxed_distribution_target = (
        particle_concentration / (math.pi * thermal_level) * jnp.exp(-kinetic_content_sum)
    )
    multiplier_coefficient = (
        (1.0 - diffusivity_ratio)
        * 0.8
        * (
            relative_speed_horizontal * thermal_current_horizontal
            + relative_speed_vertical * thermal_current_vertical
        )
        / (particle_concentration * thermal_level * thermal_level)
    )
    linear_integral_term = relaxed_distribution_target * (
        1.0 + multiplier_coefficient * (kinetic_content_sum - 2.0)
    )
    quadratic_integral_term = (
        0.5
        * thermal_level
        * relaxed_distribution_target
        * (1.0 + multiplier_coefficient * (kinetic_content_sum - 1.0))
    )
    return jnp.stack([linear_integral_term, quadratic_integral_term])


def advance(state, ghosts, neighbours, speed_x, speed_y, macroscopic_quantities):
    lower_one, lower_two, upper_one, upper_two = ghosts
    left_two, left_one, right_one, right_two = neighbours
    total = state.shape[-1]
    row_pos = jnp.arange(total, dtype=jnp.int32) % Y

    def spread(ghost):
        return jnp.repeat(ghost, Y, axis=-1)

    down_one = jnp.where(row_pos >= 1, shift_flat(state, 1), spread(lower_one))
    down_two = jnp.where(
        row_pos >= 2,
        shift_flat(state, 2),
        jnp.where(row_pos == 1, spread(lower_one), spread(lower_two)),
    )
    up_one = jnp.where(row_pos <= Y - 2, shift_flat(state, -1), spread(upper_one))
    up_two = jnp.where(
        row_pos <= Y - 3,
        shift_flat(state, -2),
        jnp.where(row_pos == Y - 2, spread(upper_one), spread(upper_two)),
    )
    along_x = speed_x[None, None, :, None]
    along_y = speed_y[None, :, None, None]
    first_x = jnp.where(along_x > 0, left_one, right_one)
    second_x = jnp.where(along_x > 0, left_two, right_two)
    first_y = jnp.where(along_y > 0, down_one, up_one)
    second_y = jnp.where(along_y > 0, down_two, up_two)
    particle_concentration = macroscopic_quantities[0]
    thermal_level = macroscopic_quantities[3]
    relaxation_frequency = (
        time_increment
        * relaxation_multiplier
        * particle_concentration
        * jnp.power(thermal_level, shear_exponent)
    )
    target = shakhov_target(speed_x, speed_y, macroscopic_quantities)
    moved = state + beam_term(state, first_x, second_x, jnp.abs(along_x) * time_increment)
    moved = moved + beam_term(state, first_y, second_y, jnp.abs(along_y) * time_increment)
    return moved + relaxation_frequency * (target - state)


def wall_tables(wall_type, wall_temp_index, wall_temps, accommodation):
    type_hits = wall_type[..., None] == jnp.arange(NTYPE, dtype=jnp.int32)
    alpha = jnp.sum(jnp.where(type_hits, accommodation.astype(jnp.float32), 0.0), axis=-1) / 100.0
    temp_hits = wall_temp_index[..., None] == jnp.arange(NTEMP, dtype=jnp.int32)
    wall_heat = jnp.sum(jnp.where(temp_hits, wall_temps, 0.0), axis=-1)
    grid_x = speeds(SPEED_NODES_HORIZ)
    grid_y = speeds(SPEED_NODES_VERT)
    kinetic_content_sum = grid_y[:, None] * grid_y[:, None] + grid_x[None, :] * grid_x[None, :]
    temps = wall_temps[:, None, None]
    flux_in = cell_weight() * jnp.sum(
        jnp.maximum(grid_y, 0.0)[None, :, None]
        * jnp.exp(-kinetic_content_sum[None] / temps)
        / (math.pi * temps),
        axis=(1, 2),
    )
    denom = jnp.sum(jnp.where(temp_hits, flux_in, 0.0), axis=-1)
    return (alpha, wall_heat, denom)


def wall_ghost(alpha, wall_heat, wall_density, mirrored, speed_x, speed_y):
    kinetic_content_sum = (
        speed_y[:, None, None] * speed_y[:, None, None]
        + speed_x[None, :, None] * speed_x[None, :, None]
    )
    gaussian_distribution = jnp.exp(-kinetic_content_sum / wall_heat) / (math.pi * wall_heat)
    diffuse = jnp.stack(
        [
            wall_density * gaussian_distribution,
            0.5 * wall_heat * wall_density * gaussian_distribution,
        ]
    )
    return alpha * diffuse + (1.0 - alpha) * mirrored


def wall_flux(dens_g, speed_y):
    bottom = jnp.sum(jnp.maximum(-speed_y, 0.0)[:, None, None] * dens_g[..., 0::Y], axis=(0, 1))
    top = jnp.sum(jnp.maximum(speed_y, 0.0)[:, None, None] * dens_g[..., Y - 1 :: Y], axis=(0, 1))
    return cell_weight() * jnp.stack([bottom, top])


def velocity_bases(speed_x, speed_y):
    grid_x = jnp.broadcast_to(speed_x[None, :], (speed_y.shape[0], speed_x.shape[0]))
    grid_y = jnp.broadcast_to(speed_y[:, None], grid_x.shape)
    return (grid_x, grid_y, jnp.ones_like(grid_x), jnp.zeros_like(grid_x))


def raw_moments(state, speed_x, speed_y):
    grid_x, grid_y, ones, zeros = velocity_bases(speed_x, speed_y)
    square = grid_x * grid_x + grid_y * grid_y
    basis_g = jnp.stack(
        [
            ones,
            grid_x,
            grid_y,
            square,
            grid_x * grid_x,
            grid_x * grid_y,
            grid_y * grid_y,
            grid_x * square,
            grid_y * square,
        ]
    )
    basis_h = jnp.stack([zeros, zeros, zeros, ones, zeros, zeros, zeros, grid_x, grid_y])
    part_g = jnp.einsum("kji,jic->kc", basis_g, state[0], precision=highest)
    part_h = jnp.einsum("kji,jic->kc", basis_h, state[1], precision=highest)
    return cell_weight() * (part_g + part_h)


def heat_from_raw(raw):
    (
        particle_concentration,
        mom_x,
        mom_y,
        kinetic_content_sum,
        press_xx,
        press_xy,
        press_yy,
        third_x,
        third_y,
    ) = (raw[0], raw[1], raw[2], raw[3], raw[4], raw[5], raw[6], raw[7], raw[8])
    bulk_flow_horizontal = mom_x / particle_concentration
    bulk_flow_vertical = mom_y / particle_concentration
    speed_sq = bulk_flow_horizontal * bulk_flow_horizontal + bulk_flow_vertical * bulk_flow_vertical
    along = bulk_flow_horizontal * mom_x + bulk_flow_vertical * mom_y
    thermal_current_horizontal = (
        third_x
        - 2.0 * (bulk_flow_horizontal * press_xx + bulk_flow_vertical * press_xy)
        + speed_sq * mom_x
        - bulk_flow_horizontal * kinetic_content_sum
        + 2.0 * bulk_flow_horizontal * along
        - bulk_flow_horizontal * speed_sq * particle_concentration
    )
    thermal_current_vertical = (
        third_y
        - 2.0 * (bulk_flow_horizontal * press_xy + bulk_flow_vertical * press_yy)
        + speed_sq * mom_y
        - bulk_flow_vertical * kinetic_content_sum
        + 2.0 * bulk_flow_vertical * along
        - bulk_flow_vertical * speed_sq * particle_concentration
    )
    return jnp.stack([thermal_current_horizontal, thermal_current_vertical])


def macro_fields(invariant_quantities, thermal_current_pair):
    particle_concentration = invariant_quantities[0]
    bulk_flow_horizontal = invariant_quantities[1] / particle_concentration
    bulk_flow_vertical = invariant_quantities[2] / particle_concentration
    thermal_level = (
        2.0
        / 3.0
        * (
            invariant_quantities[3] / particle_concentration
            - bulk_flow_horizontal * bulk_flow_horizontal
            - bulk_flow_vertical * bulk_flow_vertical
        )
    )
    return (
        particle_concentration,
        bulk_flow_horizontal,
        bulk_flow_vertical,
        thermal_level,
        thermal_current_pair[0],
        thermal_current_pair[1],
    )


def on_device(distribution, wall_type, wall_temp_index, wall_temps, accommodation):
    vert_index = lax.axis_index("vert")
    band_rows = distribution.shape[1]
    speed_x = speeds(SPEED_NODES_HORIZ)
    speed_y = band_speeds(vert_index, band_rows)
    alpha, wall_heat, denom = wall_tables(wall_type, wall_temp_index, wall_temps, accommodation)
    upper_half = vert_index % 2 == 1
    state = distribution
    for iteration in range(ITERS):
        total = state.shape[-1]
        columns = total // Y
        padded = with_halo(state, (("gx", 3),), 2 * Y)
        neighbours = (
            padded[..., 0:total],
            padded[..., Y : Y + total],
            padded[..., 3 * Y : 3 * Y + total],
            padded[..., 4 * Y : 4 * Y + total],
        )
        bottom_rows = jnp.stack([state[..., 0::Y], state[..., 1::Y]])
        top_rows = jnp.stack([state[..., Y - 1 :: Y], state[..., Y - 2 :: Y]])
        payload = jnp.where(upper_half, top_rows, bottom_rows).reshape(
            2, 2, band_rows, SPEED_NODES_HORIZ * columns
        )
        received = swapped(payload, "vert", 0)
        mirrored = received.reshape(2, 2, band_rows, SPEED_NODES_HORIZ, columns)
        flux_part = wall_flux(state[0], speed_y)
        raw, flux = lax.psum((raw_moments(state, speed_x, speed_y), flux_part), "vert")
        invariant_quantities = raw[0:4]
        thermal_current_pair = heat_from_raw(raw)
        macroscopic_quantities = macro_fields(invariant_quantities, thermal_current_pair)
        wall_density = flux / denom
        ghosts = (
            wall_ghost(alpha[0], wall_heat[0], wall_density[0], mirrored[0], speed_x, speed_y),
            wall_ghost(alpha[0], wall_heat[0], wall_density[0], mirrored[1], speed_x, speed_y),
            wall_ghost(alpha[1], wall_heat[1], wall_density[1], mirrored[0], speed_x, speed_y),
            wall_ghost(alpha[1], wall_heat[1], wall_density[1], mirrored[1], speed_x, speed_y),
        )
        state = advance(state, ghosts, neighbours, speed_x, speed_y, macroscopic_quantities)
    return state


def solution(mesh):
    placed = (P(None, "vert", None, "gx"), P(None, "gx"), P(None, "gx"), P(), P())
    return jax.shard_map(
        on_device,
        mesh=mesh,
        in_specs=placed,
        out_specs=P(None, "vert", None, "gx"),
        check_vma=False,
    )
```

profile of v0, /device:TPU:0, one launch (start us, length us, event | category | flops | bytes accessed | tf_op | source)
XLA Modules:
  0.0 583.2 jit_solution(14696571091720847422)
XLA Ops:
  0.0 12.0 %slice.507 = f32[2,24,96,8]{3,2,1,0:T(8,128)} slice(f32[2,24,96,128]{3,2,1,0:T(8,128)} %param.5), slice={[0:2:1], [0:24:1], [0:96:1], [0:128:16]} | slice | bytes 294912 | tf_op jit(solution)/shard_map/slice | solution.py:304
  12.0 8.7 %slice.506 = f32[2,24,96,8]{3,2,1,0:T(8,128)} slice(f32[2,24,96,128]{3,2,1,0:T(8,128)S(1)} %copy-done.2), slice={[0:2:1], [0:24:1], [0:96:1], [14:128:16]} | slice | bytes 294912 | tf_op jit(solution)/shard_map/slice | solution.py:305
  20.7 8.7 %slice.505 = f32[2,24,96,8]{3,2,1,0:T(8,128)} slice(f32[2,24,96,128]{3,2,1,0:T(8,128)S(1)} %copy-done.2), slice={[0:2:1], [0:24:1], [0:96:1], [15:128:16]} | slice | bytes 294912 | tf_op jit(solution)/shard_map/slice | solution.py:305
  29.5 8.7 %slice.508 = f32[2,24,96,8]{3,2,1,0:T(8,128)} slice(f32[2,24,96,128]{3,2,1,0:T(8,128)S(1)} %copy-done.2), slice={[0:2:1], [0:24:1], [0:96:1], [1:128:16]} | slice | bytes 294912 | tf_op jit(solution)/shard_map/slice | solution.py:304
  52.8 3.1 collective-permute-start.2
  55.8 3.0 fusion.131
  58.9 3.2 copy.374
  63.7 3.2 copy.373
  73.1 4.6 slice.502
  77.7 4.4 slice.501
  99.7 11.4 %all-reduce.19 = (f32[9,128]{1,0:T(8,128)S(1)}, f32[2,8]{1,0:T(2,128)S(1)}) all-reduce(f32[9,128]{1,0:T(8,128)S(1)} %fusion.37, f32[2,8]{1,0:T(2,128)S(1)} %maximum_multiply_fusion.8), channel_id=1, replica_groups=mesh['gx'=8,'vert'=4] {'vert'}, use_global_device_ids=true, to_apply=%region_7.8 | all-reduce | flops 1168 | bytes 9344 | tf_op jit(solution)/shard_map/psum | solution.py:312
  111.2 3.0 fusion.132
  135.7 3.2 copy.271
  139.0 3.2 copy.273
  142.4 16.6 %fusion.17 = f32[2,24,96,128]{3,2,1,0:T(8,128)S(1)} fusion(f32[2,24,96,128]{3,2,1,0:T(8,128)} %param.5, f32[1,24,96,128]{3,2,1,0:T(8,128)} %get-tuple-element.96, f32[1,24,96,128]{3,2,1,0:T(8,128)} %get-tuple-element.95, f32[2,24,96,128]{3,2,1,0:T(8,128)} %copy.286, f32[2,24,96,128]{3,2,1,0:T(8,128)} %copy.293, f32[2,24,96,126]{3,2,1,0:T(8,128)} %get-tuple-element.56, ...), kind=kLoop, calls=%fused_computation.42 | loop fusion | flops 23003136 | bytes 27023672 | tf_op jit(solution)/shard_map/add | solution.py:157
  160.8 4.6 slice.536
  165.4 4.4 slice.535
  169.8 8.8 %slice.539 = f32[2,24,96,8]{3,2,1,0:T(8,128)} slice(f32[2,24,96,128]{3,2,1,0:T(8,128)S(1)} %fusion.17), slice={[0:2:1], [0:24:1], [0:96:1], [14:128:16]} | slice | bytes 294912 | tf_op jit(solution)/shard_map/slice | solution.py:305
  178.5 8.8 %slice.538 = f32[2,24,96,8]{3,2,1,0:T(8,128)} slice(f32[2,24,96,128]{3,2,1,0:T(8,128)S(1)} %fusion.17), slice={[0:2:1], [0:24:1], [0:96:1], [15:128:16]} | slice | bytes 294912 | tf_op jit(solution)/shard_map/slice | solution.py:305
  187.3 8.8 %slice.541 = f32[2,24,96,8]{3,2,1,0:T(8,128)} slice(f32[2,24,96,128]{3,2,1,0:T(8,128)S(1)} %fusion.17), slice={[0:2:1], [0:24:1], [0:96:1], [1:128:16]} | slice | bytes 294912 | tf_op jit(solution)/shard_map/slice | solution.py:304
  196.1 16.9 %slice.540 = f32[2,24,96,8]{3,2,1,0:T(8,128)} slice(f32[2,24,96,128]{3,2,1,0:T(8,128)S(1)} %fusion.17), slice={[0:2:1], [0:24:1], [0:96:1], [0:128:16]} | slice | bytes 294912 | tf_op jit(solution)/shard_map/slice | solution.py:304
  216.0 3.0 fusion.128
  219.0 3.0 fusion.130
  224.1 8.8 %all-reduce.18 = (f32[9,128]{1,0:T(8,128)S(1)}, f32[2,8]{1,0:T(2,128)S(1)}) all-reduce(f32[9,128]{1,0:T(8,128)S(1)} %fusion.39, f32[2,8]{1,0:T(2,128)S(1)} %maximum_multiply_fusion.9), channel_id=1, replica_groups=mesh['gx'=8,'vert'=4] {'vert'}, use_global_device_ids=true, to_apply=%region_11.12 | all-reduce | flops 1168 | bytes 9344 | tf_op jit(solution)/shard_map/psum | solution.py:312
  247.6 3.0 add_multiply_fusion.5
  251.3 3.2 copy.298
  269.9 6.4 %collective-permute-done.3 = f32[2,24,96,32]{2,3,1,0:T(8,128)} collective-permute-done((f32[2,24,96,32]{2,3,1,0:T(8,128)}, f32[2,24,96,32]{2,3,1,0:T(8,128)}, u32[]{:S(2)}, u32[]{:S(2)}) %collective-permute-start.3) | collective-permute-done | bytes 589856 | tf_op jit(solution)/shard_map/ppermute | solution.py:32
  276.3 3.2 copy.299
  279.5 3.4 copy.301
  282.9 16.1 %fusion.19 = f32[2,24,96,128]{3,2,1,0:T(8,128)S(1)} fusion(f32[2,24,96,128]{3,2,1,0:T(8,128)} %copy-done.1, f32[1,24,96,128]{3,2,1,0:T(8,128)} %get-tuple-element.94, f32[1,24,96,128]{3,2,1,0:T(8,128)S(1)} %copy-done.15, f32[2,24,96,128]{3,2,1,0:T(8,128)} %copy.314, f32[2,24,96,128]{3,2,1,0:T(8,128)} %copy.321, f32[2,24,96,126]{3,2,1,0:T(8,128)} %get-tuple-element.50, ...), kind=kLoop, calls=%fused_computation.45 | loop fusion | flops 23003136 | bytes 27023672 | tf_op jit(solution)/shard_map/add | solution.py:157
  300.8 4.6 slice.567
  305.4 4.4 slice.566
  309.8 8.8 %slice.570 = f32[2,24,96,8]{3,2,1,0:T(8,128)} slice(f32[2,24,96,128]{3,2,1,0:T(8,128)S(1)} %fusion.19), slice={[0:2:1], [0:24:1], [0:96:1], [14:128:16]} | slice | bytes 294912 | tf_op jit(solution)/shard_map/slice | solution.py:305
  318.5 8.8 %slice.569 = f32[2,24,96,8]{3,2,1,0:T(8,128)} slice(f32[2,24,96,128]{3,2,1,0:T(8,128)S(1)} %fusion.19), slice={[0:2:1], [0:24:1], [0:96:1], [15:128:16]} | slice | bytes 294912 | tf_op jit(solution)/shard_map/slice | solution.py:305
  327.3 8.8 %slice.572 = f32[2,24,96,8]{3,2,1,0:T(8,128)} slice(f32[2,24,96,128]{3,2,1,0:T(8,128)S(1)} %fusion.19), slice={[0:2:1], [0:24:1], [0:96:1], [1:128:16]} | slice | bytes 294912 | tf_op jit(solution)/shard_map/slice | solution.py:304
  336.1 8.8 %slice.571 = f32[2,24,96,8]{3,2,1,0:T(8,128)} slice(f32[2,24,96,128]{3,2,1,0:T(8,128)S(1)} %fusion.19), slice={[0:2:1], [0:24:1], [0:96:1], [0:128:16]} | slice | bytes 294912 | tf_op jit(solution)/shard_map/slice | solution.py:304
  347.9 3.0 fusion.125
  350.9 3.0 fusion.127
  356.0 9.0 %all-reduce.17 = (f32[9,128]{1,0:T(8,128)S(1)}, f32[2,8]{1,0:T(2,128)S(1)}) all-reduce(f32[9,128]{1,0:T(8,128)S(1)} %fusion.41, f32[2,8]{1,0:T(2,128)S(1)} %maximum_multiply_fusion.10), channel_id=1, replica_groups=mesh['gx'=8,'vert'=4] {'vert'}, use_global_device_ids=true, to_apply=%region_15.16 | all-reduce | flops 1168 | bytes 9344 | tf_op jit(solution)/shard_map/psum | solution.py:312
  379.5 3.0 add_multiply_fusion.3
  383.3 3.2 copy.323
  401.8 5.8 collective-permute-done.6
  407.6 3.2 copy.324
  410.8 3.4 copy.326
  414.2 16.1 %fusion.21 = f32[2,24,96,128]{3,2,1,0:T(8,128)S(1)} fusion(f32[2,24,96,128]{3,2,1,0:T(8,128)} %copy-done, f32[1,24,96,128]{3,2,1,0:T(8,128)} %get-tuple-element.92, f32[1,24,96,128]{3,2,1,0:T(8,128)S(1)} %copy-done.16, f32[2,24,96,128]{3,2,1,0:T(8,128)} %copy.339, f32[2,24,96,128]{3,2,1,0:T(8,128)} %copy.346, f32[2,24,96,126]{3,2,1,0:T(8,128)} %get-tuple-element.44, ...), kind=kLoop, calls=%fused_computation.48 | loop fusion | flops 23003136 | bytes 27023672 | tf_op jit(solution)/shard_map/add | solution.py:157
  432.1 4.6 slice.598
  436.7 4.4 slice.597
  441.1 8.7 %slice.601 = f32[2,24,96,8]{3,2,1,0:T(8,128)} slice(f32[2,24,96,128]{3,2,1,0:T(8,128)S(1)} %fusion.21), slice={[0:2:1], [0:24:1], [0:96:1], [14:128:16]} | slice | bytes 294912 | tf_op jit(solution)/shard_map/slice | solution.py:305
  449.8 8.8 %slice.600 = f32[2,24,96,8]{3,2,1,0:T(8,128)} slice(f32[2,24,96,128]{3,2,1,0:T(8,128)S(1)} %fusion.21), slice={[0:2:1], [0:24:1], [0:96:1], [15:128:16]} | slice | bytes 294912 | tf_op jit(solution)/shard_map/slice | solution.py:305
  458.6 8.8 %slice.603 = f32[2,24,96,8]{3,2,1,0:T(8,128)} slice(f32[2,24,96,128]{3,2,1,0:T(8,128)S(1)} %fusion.21), slice={[0:2:1], [0:24:1], [0:96:1], [1:128:16]} | slice | bytes 294912 | tf_op jit(solution)/shard_map/slice | solution.py:304
  467.3 8.6 %slice.602 = f32[2,24,96,8]{3,2,1,0:T(8,128)} slice(f32[2,24,96,128]{3,2,1,0:T(8,128)S(1)} %fusion.21), slice={[0:2:1], [0:24:1], [0:96:1], [0:128:16]} | slice | bytes 294912 | tf_op jit(solution)/shard_map/slice | solution.py:304
  475.9 3.1 fusion.123
  479.0 3.0 fusion.122
  482.1 3.0 fusion.124
  486.8 9.0 %all-reduce.16 = (f32[9,128]{1,0:T(8,128)S(1)}, f32[2,8]{1,0:T(2,128)S(1)}) all-reduce(f32[9,128]{1,0:T(8,128)S(1)} %fusion.43, f32[2,8]{1,0:T(2,128)S(1)} %maximum_multiply_fusion.11), channel_id=1, replica_groups=mesh['gx'=8,'vert'=4] {'vert'}, use_global_device_ids=true, to_apply=%region_19.20 | all-reduce | flops 1168 | bytes 9344 | tf_op jit(solution)/shard_map/psum | solution.py:312
  518.2 3.2 copy.348
  521.5 3.2 copy.350
  540.8 3.6 copy.371
  547.2 3.4 copy.364
  553.4 3.3 copy.362
  559.6 3.4 copy.368
  563.0 3.2 copy.349
  566.2 3.3 copy.351
  569.5 13.2 %fusion.23 = f32[2,24,96,128]{3,2,1,0:T(8,128)} fusion(f32[2,24,96,128]{3,2,1,0:T(8,128)S(1)} %fusion.21, f32[1,24,96,128]{3,2,1,0:T(8,128)} %get-tuple-element.90, f32[1,24,96,128]{3,2,1,0:T(8,128)S(1)} %get-tuple-element.89, f32[2,24,96,128]{3,2,1,0:T(8,128)} %copy.364, f32[2,24,96,128]{3,2,1,0:T(8,128)} %copy.371, ...), kind=kLoop, calls=%fused_computation.51 | loop fusion | flops 23003136 | bytes 27023672 | tf_op jit(solution)/shard_map/add | solution.py:157
  (424 shorter events, 186.0 us)
Async XLA Ops:
  0.0 12.0 %copy-start.2 = (f32[2,24,96,128]{3,2,1,0:T(8,128)S(1)}, f32[2,24,96,128]{3,2,1,0:T(8,128)}, u32[]{:S(2)}) copy-start(f32[2,24,96,128]{3,2,1,0:T(8,128)} %param.5) | copy-start | bytes 7077892
  52.8 68.2 %collective-permute-start.2 = (f32[2,2,24,768]{3,2,1,0:T(8,128)}, f32[2,2,24,768]{3,2,1,0:T(8,128)}, u32[]{:S(2)}, u32[]{:S(2)}) collective-permute-start(f32[2,2,24,768]{3,2,1,0:T(8,128)} %maximum_select_fusion), channel_id=1, source_target_pairs={{0,1},{1,0},{2,3},{3,2},{4,5},{5,4},{6,7},{7,6},{8,9},{9,8},{10,11... | collective-permute-start | bytes 884744 | tf_op jit(solution)/shard_map/ppermute | solution.py:44
  62.1 77.0 %collective-permute-start.1 = (f32[2,24,96,32]{2,3,1,0:T(8,128)}, f32[2,24,96,32]{2,3,1,0:T(8,128)}, u32[]{:S(2)}, u32[]{:S(2)}) collective-permute-start(f32[2,24,96,32]{2,3,1,0:T(8,128)} %copy.374), channel_id=1, source_target_pairs={{4,0},{8,4},{12,8},{16,12},{20,16},{24,20},{28,24},{0,28},{5,1},{9... | collective-permute-start | bytes 1769480 | tf_op jit(solution)/shard_map/ppermute | solution.py:34
  66.9 68.9 %collective-permute-start = (f32[2,24,96,32]{2,3,1,0:T(8,128)}, f32[2,24,96,32]{2,3,1,0:T(8,128)}, u32[]{:S(2)}, u32[]{:S(2)}) collective-permute-start(f32[2,24,96,32]{2,3,1,0:T(8,128)} %copy.373), channel_id=1, source_target_pairs={{0,4},{4,8},{8,12},{12,16},{16,20},{20,24},{24,28},{28,0},{1,5},{5... | collective-permute-start | bytes 1769480 | tf_op jit(solution)/shard_map/ppermute | solution.py:32
  67.4 15.9 %copy-start.40 = (f32[96]{0:T(128)}, f32[96]{0:T(128)S(1)}, u32[]{:S(2)}) copy-start(f32[96]{0:T(128)S(1)} %fusion.97) | copy-start | bytes 1156
  73.1 9.0 %copy-start.102 = (f32[2]{0:T(128)S(1)}, f32[2]{0:T(128)}, u32[]{:S(2)}) copy-start(f32[2]{0:T(128)} %param.8) | copy-start | bytes 28
  83.3 16.4 %copy-start.76 = (f32[24]{0:T(128)}, f32[24]{0:T(128)S(1)}, u32[]{:S(2)}) copy-start(f32[24]{0:T(128)S(1)} %get-tuple-element.195) | copy-start | bytes 292
  83.3 16.4 %copy-start.80 = (f32[24]{0:T(128)}, f32[24]{0:T(128)S(1)}, u32[]{:S(2)}) copy-start(f32[24]{0:T(128)S(1)} %get-tuple-element.196) | copy-start | bytes 292
  85.8 25.4 %copy-start.36 = (f32[2,8]{1,0:T(2,128)}, f32[2,8]{1,0:T(2,128)S(1)}, u32[]{:S(2)}) copy-start(f32[2,8]{1,0:T(2,128)S(1)} %get-tuple-element.6) | copy-start | bytes 196
  85.8 25.4 %copy-start.25 = (f32[2,8]{1,0:T(2,128)}, f32[2,8]{1,0:T(2,128)S(1)}, u32[]{:S(2)}) copy-start(f32[2,8]{1,0:T(2,128)S(1)} %get-tuple-element.5) | copy-start | bytes 196
  85.8 34.4 %copy-start.47 = (f32[8]{0:T(128)}, f32[8]{0:T(128)S(1)}, u32[]{:S(2)}) copy-start(f32[8]{0:T(128)S(1)} %get-tuple-element.179) | copy-start | bytes 100
  85.8 34.4 %copy-start.51 = (f32[8]{0:T(128)}, f32[8]{0:T(128)S(1)}, u32[]{:S(2)}) copy-start(f32[8]{0:T(128)S(1)} %get-tuple-element.180) | copy-start | bytes 100
  95.7 63.3 %copy-start.12 = (f32[9,24,96]{2,0,1:T(8,128)}, f32[9,24,96]{2,0,1:T(8,128)S(1)}, u32[]{:S(2)}) copy-start(f32[9,24,96]{2,0,1:T(8,128)S(1)} %stack.112) | copy-start | bytes 248836
  95.7 3.5 copy-start.17
  111.2 9.0 %copy-start.70 = (f32[8]{0:T(128)}, f32[8]{0:T(128)S(1)}, u32[]{:S(2)}) copy-start(f32[8]{0:T(128)S(1)} %get-tuple-element.181) | copy-start | bytes 100
  111.2 9.0 %copy-start.73 = (f32[8]{0:T(128)}, f32[8]{0:T(128)S(1)}, u32[]{:S(2)}) copy-start(f32[8]{0:T(128)S(1)} %get-tuple-element.182) | copy-start | bytes 100
  114.3 3.7 copy-start.32
  117.4 5.8 copy-start.54
  117.4 5.8 copy-start.58
  120.4 3.7 copy-start.62
  120.4 3.7 copy-start.66
  159.0 63.0 %copy-start.1 = (f32[2,24,96,128]{3,2,1,0:T(8,128)}, f32[2,24,96,128]{3,2,1,0:T(8,128)S(1)}, u32[]{:S(2)}) copy-start(f32[2,24,96,128]{3,2,1,0:T(8,128)S(1)} %fusion.17) | copy-start | bytes 7077892
  219.0 4.2 copy-start.21
  219.0 4.2 copy-start.77
  222.1 10.8 %copy-start.37 = (f32[2,8]{1,0:T(2,128)S(1)}, f32[2,8]{1,0:T(2,128)}, u32[]{:S(2)}) copy-start(f32[2,8]{1,0:T(2,128)} %copy-done.36) | copy-start | bytes 196
  222.1 10.9 %copy-start.26 = (f32[2,8]{1,0:T(2,128)S(1)}, f32[2,8]{1,0:T(2,128)}, u32[]{:S(2)}) copy-start(f32[2,8]{1,0:T(2,128)} %copy-done.25) | copy-start | bytes 196
  222.1 13.3 %copy-start.33 = (f32[96]{0:T(128)S(1)}, f32[96]{0:T(128)}, u32[]{:S(2)}) copy-start(f32[96]{0:T(128)} %add_multiply_fusion.11) | copy-start | bytes 1156
  224.0 14.3 %copy-start.5 = (f32[2,24,96,8]{3,2,1,0:T(8,128)S(1)}, f32[2,24,96,8]{3,2,1,0:T(8,128)}, u32[]{:S(2)}) copy-start(f32[2,24,96,8]{3,2,1,0:T(8,128)} %slice.538) | copy-start | bytes 442372
  239.5 3.9 copy-start.3
  245.7 11.2 %collective-permute-start.5 = (f32[2,2,24,768]{3,2,1,0:T(8,128)S(1)}, f32[2,2,24,768]{3,2,1,0:T(8,128)S(1)}, u32[]{:S(2)}, u32[]{:S(2)}) collective-permute-start(f32[2,2,24,768]{3,2,1,0:T(8,128)S(1)} %maximum_select_fusion.1), channel_id=1, source_target_pairs={{0,1},{1,0},{2,3},{3,2},{4,5},{5,4},{6,7},{7,6},{8,9},{9,8},{10,11... | collective-permute-start | bytes 884744 | tf_op jit(solution)/shard_map/ppermute | solution.py:44
  247.6 7.0 %copy-start.7 = (f32[2,24,96,32]{3,2,1,0:T(8,128)S(1)}, f32[2,24,96,32]{3,2,1,0:T(8,128)}, u32[]{:S(2)}) copy-start(f32[2,24,96,32]{3,2,1,0:T(8,128)} %get-tuple-element.46) | copy-start | bytes 1769476
  256.2 23.4 %collective-permute-start.4 = (f32[2,24,96,32]{2,3,1,0:T(8,128)}, f32[2,24,96,32]{2,3,1,0:T(8,128)}, u32[]{:S(2)}, u32[]{:S(2)}) collective-permute-start(f32[2,24,96,32]{2,3,1,0:T(8,128)} %copy.300), channel_id=1, source_target_pairs={{4,0},{8,4},{12,8},{16,12},{20,16},{24,20},{28,24},{0,28},{5,1},{9... | collective-permute-start | bytes 1769480 | tf_op jit(solution)/shard_map/ppermute | solution.py:34
  256.2 20.1 %collective-permute-start.3 = (f32[2,24,96,32]{2,3,1,0:T(8,128)}, f32[2,24,96,32]{2,3,1,0:T(8,128)}, u32[]{:S(2)}, u32[]{:S(2)}) collective-permute-start(f32[2,24,96,32]{2,3,1,0:T(8,128)} %copy.298), channel_id=1, source_target_pairs={{0,4},{4,8},{8,12},{12,16},{16,20},{20,24},{24,28},{28,0},{1,5},{5... | collective-permute-start | bytes 1769480 | tf_op jit(solution)/shard_map/ppermute | solution.py:32
  282.9 16.1 %copy-start.13 = (f32[9,24,96]{2,0,1:T(8,128)S(1)}, f32[9,24,96]{2,0,1:T(8,128)}, u32[]{:S(2)}) copy-start(f32[9,24,96]{2,0,1:T(8,128)} %copy-done.12) | copy-start | bytes 248836
  299.0 54.9 %copy-start = (f32[2,24,96,128]{3,2,1,0:T(8,128)}, f32[2,24,96,128]{3,2,1,0:T(8,128)S(1)}, u32[]{:S(2)}) copy-start(f32[2,24,96,128]{3,2,1,0:T(8,128)S(1)} %fusion.19) | copy-start | bytes 7077892
  350.9 4.2 copy-start.22
  350.9 4.2 copy-start.78
  354.0 11.0 %copy-start.38 = (f32[2,8]{1,0:T(2,128)S(1)}, f32[2,8]{1,0:T(2,128)}, u32[]{:S(2)}) copy-start(f32[2,8]{1,0:T(2,128)} %copy-done.36) | copy-start | bytes 196
  354.0 11.0 %copy-start.27 = (f32[2,8]{1,0:T(2,128)S(1)}, f32[2,8]{1,0:T(2,128)}, u32[]{:S(2)}) copy-start(f32[2,8]{1,0:T(2,128)} %copy-done.25) | copy-start | bytes 196
  354.0 13.5 %copy-start.34 = (f32[96]{0:T(128)S(1)}, f32[96]{0:T(128)}, u32[]{:S(2)}) copy-start(f32[96]{0:T(128)} %add_multiply_fusion.11) | copy-start | bytes 1156
  356.0 14.5 %copy-start.6 = (f32[2,24,96,8]{3,2,1,0:T(8,128)S(1)}, f32[2,24,96,8]{3,2,1,0:T(8,128)}, u32[]{:S(2)}) copy-start(f32[2,24,96,8]{3,2,1,0:T(8,128)} %slice.569) | copy-start | bytes 442372
  371.6 3.9 copy-start.4
  377.8 11.0 %collective-permute-start.8 = (f32[2,2,24,768]{3,2,1,0:T(8,128)S(1)}, f32[2,2,24,768]{3,2,1,0:T(8,128)S(1)}, u32[]{:S(2)}, u32[]{:S(2)}) collective-permute-start(f32[2,2,24,768]{3,2,1,0:T(8,128)S(1)} %maximum_select_fusion.2), channel_id=1, source_target_pairs={{0,1},{1,0},{2,3},{3,2},{4,5},{5,4},{6,7},{7,6},{8,9},{9,8},{10,11... | collective-permute-start | bytes 884744 | tf_op jit(solution)/shard_map/ppermute | solution.py:44
  379.5 7.0 %copy-start.8 = (f32[2,24,96,32]{3,2,1,0:T(8,128)S(1)}, f32[2,24,96,32]{3,2,1,0:T(8,128)}, u32[]{:S(2)}) copy-start(f32[2,24,96,32]{3,2,1,0:T(8,128)} %get-tuple-element.40) | copy-start | bytes 1769476
  388.1 22.7 %collective-permute-start.7 = (f32[2,24,96,32]{2,3,1,0:T(8,128)}, f32[2,24,96,32]{2,3,1,0:T(8,128)}, u32[]{:S(2)}, u32[]{:S(2)}) collective-permute-start(f32[2,24,96,32]{2,3,1,0:T(8,128)} %copy.325), channel_id=1, source_target_pairs={{4,0},{8,4},{12,8},{16,12},{20,16},{24,20},{28,24},{0,28},{5,1},{9... | collective-permute-start | bytes 1769480 | tf_op jit(solution)/shard_map/ppermute | solution.py:34
  388.1 19.5 %collective-permute-start.6 = (f32[2,24,96,32]{2,3,1,0:T(8,128)}, f32[2,24,96,32]{2,3,1,0:T(8,128)}, u32[]{:S(2)}, u32[]{:S(2)}) collective-permute-start(f32[2,24,96,32]{2,3,1,0:T(8,128)} %copy.323), channel_id=1, source_target_pairs={{0,4},{4,8},{8,12},{12,16},{16,20},{20,24},{24,28},{28,0},{1,5},{5... | collective-permute-start | bytes 1769480 | tf_op jit(solution)/shard_map/ppermute | solution.py:32
  410.8 3.4 copy-start.16
  414.2 16.1 %copy-start.14 = (f32[9,24,96]{2,0,1:T(8,128)S(1)}, f32[9,24,96]{2,0,1:T(8,128)}, u32[]{:S(2)}) copy-start(f32[9,24,96]{2,0,1:T(8,128)} %copy-done.12) | copy-start | bytes 248836
  482.1 4.2 copy-start.23
  482.1 4.2 copy-start.24
  482.1 4.2 copy-start.79
  482.1 4.2 copy-start.83
  485.1 10.7 %copy-start.39 = (f32[2,8]{1,0:T(2,128)S(1)}, f32[2,8]{1,0:T(2,128)}, u32[]{:S(2)}) copy-start(f32[2,8]{1,0:T(2,128)} %copy-done.36) | copy-start | bytes 196
  485.1 10.7 %copy-start.28 = (f32[2,8]{1,0:T(2,128)S(1)}, f32[2,8]{1,0:T(2,128)}, u32[]{:S(2)}) copy-start(f32[2,8]{1,0:T(2,128)} %copy-done.25) | copy-start | bytes 196
  485.1 13.1 %copy-start.35 = (f32[96]{0:T(128)S(1)}, f32[96]{0:T(128)}, u32[]{:S(2)}) copy-start(f32[96]{0:T(128)} %add_multiply_fusion.11) | copy-start | bytes 1156
  511.0 6.8 %copy-start.85 = (f32[2,8]{1,0:T(2,128)S(1)}, f32[2,8]{1,0:T(2,128)}, u32[]{:S(2)}) copy-start(f32[2,8]{1,0:T(2,128)} %copy-done.84) | copy-start | bytes 196
  513.6 13.2 %collective-permute-start.11 = (f32[2,2,24,768]{3,2,1,0:T(8,128)}, f32[2,2,24,768]{3,2,1,0:T(8,128)}, u32[]{:S(2)}, u32[]{:S(2)}) collective-permute-start(f32[2,2,24,768]{3,2,1,0:T(8,128)} %maximum_select_fusion.3), channel_id=1, source_target_pairs={{0,1},{1,0},{2,3},{3,2},{4,5},{5,4},{6,7},{7,6},{8,9},{9,8},{10,11... | collective-permute-start | bytes 884744 | tf_op jit(solution)/shard_map/ppermute | solution.py:44
  521.5 3.7 copy-start.50
  524.7 41.6 %collective-permute-start.10 = (f32[2,24,96,32]{2,3,1,0:T(8,128)}, f32[2,24,96,32]{2,3,1,0:T(8,128)}, u32[]{:S(2)}, u32[]{:S(2)}) collective-permute-start(f32[2,24,96,32]{2,3,1,0:T(8,128)} %copy.350), channel_id=1, source_target_pairs={{4,0},{8,4},{12,8},{16,12},{20,16},{24,20},{28,24},{0,28},{5,1},{9... | collective-permute-start | bytes 1769480 | tf_op jit(solution)/shard_map/ppermute | solution.py:34
  524.7 38.3 %collective-permute-start.9 = (f32[2,24,96,32]{2,3,1,0:T(8,128)}, f32[2,24,96,32]{2,3,1,0:T(8,128)}, u32[]{:S(2)}, u32[]{:S(2)}) collective-permute-start(f32[2,24,96,32]{2,3,1,0:T(8,128)} %copy.348), channel_id=1, source_target_pairs={{0,4},{4,8},{8,12},{12,16},{16,20},{20,24},{24,28},{28,0},{1,5},{5... | collective-permute-start | bytes 1769480 | tf_op jit(solution)/shard_map/ppermute | solution.py:32
  526.7 10.0 %copy-start.57 = (f32[8]{0:T(128)S(1)}, f32[8]{0:T(128)}, u32[]{:S(2)}) copy-start(f32[8]{0:T(128)} %copy-done.54) | copy-start | bytes 100
  526.7 10.0 %copy-start.61 = (f32[8]{0:T(128)S(1)}, f32[8]{0:T(128)}, u32[]{:S(2)}) copy-start(f32[8]{0:T(128)} %copy-done.58) | copy-start | bytes 100
  526.7 10.0 %copy-start.65 = (f32[8]{0:T(128)S(1)}, f32[8]{0:T(128)}, u32[]{:S(2)}) copy-start(f32[8]{0:T(128)} %copy-done.62) | copy-start | bytes 100
  526.7 10.0 %copy-start.69 = (f32[8]{0:T(128)S(1)}, f32[8]{0:T(128)}, u32[]{:S(2)}) copy-start(f32[8]{0:T(128)} %copy-done.66) | copy-start | bytes 100
  (54 other events, 137.6 us)
where the time goes:
time: 594 us; the launch traced here: 583 us
  local copies, waits for them, and re-layouts  396 us (67%)
  other arithmetic  112 us (19%)
  blocking collectives  38.2 us (6%)
  waiting for transfers between devices  12.3 us (2%)
  starting transfers between devices  11.5 us (2%)
  matrix products  11.4 us (2%)
    slice x16, local copies, waits for them, and re-layouts, on_device(): bottom_rows = jnp.stack([state[..., 0::Y], state[..., 1::Y]])  99.7 us
    slice x16, local copies, waits for them, and re-layouts, on_device(): top_rows = jnp.stack([state[..., Y - 1::Y], state[..., Y - 2::Y]])  88.1 us
    add x4, other arithmetic, advance(): return moved + relaxation_frequency * (target - state)  62 us
    reshape x16, local copies, waits for them, and re-layouts, spread(): return jnp.repeat(ghost, Y, axis=-1)  40.6 us
    psum x4, blocking collectives, on_device(): lax.psum((raw_moments(state, speed_x, speed_y), flux_part), 'vert')  38.2 us
    slice x8, local copies, waits for them, and re-layouts, shift_flat(): return jnp.concatenate([padding, values[..., :-extent]], axis=-1)  24.1 us
    slice x7, local copies, waits for them, and re-layouts, with_halo(): lax.slice_in_dim(cells, cells.shape[dim] - width, cells.shape[dim], axis=...  21.7 us
    slice x4, local copies, waits for them, and re-layouts, wall_flux(): dens_g[..., Y - 1::Y]  18.3 us
  transfers between devices with their start and end apart: 12, of which 2 were waited for; matrix products, arithmetic and copies ran while one was open for 29% of the time, Pallas kernels for 0%

commit v1 on v0

v1 whole, which is shorter than its diff:
```python
import functools
import math

import jax
import jax.numpy as jnp
from jax import lax
from jax.experimental import pallas as pl
from jax.experimental.pallas import tpu as pltpu
from jax.sharding import PartitionSpec as P


Y = 16
ITERS = 4
NTEMP = 2
NTYPE = 3
SUB = 8
ROWS = 16

vmax_speed = 4.5
courant = 0.5
diffusivity_ratio = 2.0 / 3.0
relaxation_multiplier = 2.5
shear_exponent = 0.19
time_increment = courant / vmax_speed


class Sizes:
    def __init__(self, band, nx, cells, vert):
        self.band, self.nx, self.cells, self.vert = band, nx, cells, vert
        self.nv = band * vert
        self.groups = nx // SUB
        self.half = self.groups // 2
        self.wall_packs = -(-band // SUB)
        self.side_slots = cells // (2 * Y)
        self.side_packs = -(-band // self.side_slots)
        self.weight = 2.0 * vmax_speed / nx * (2.0 * vmax_speed / self.nv)

    def mirror_index(self, f, group, pack):
        return f * self.groups * self.wall_packs + group * self.wall_packs + pack

    @property
    def mirror_blocks(self):
        return 2 * self.groups * self.wall_packs


def lanes(sz):
    return lax.broadcasted_iota(jnp.int32, (1, sz.cells), 1)


def node_speed(index, number):
    return vmax_speed * (2.0 * index.astype(jnp.float32) + 1.0 - number) / number


def row_speed(sz, vert_index, offset):
    lower = vert_index // 2 * sz.band + offset
    return node_speed(jnp.where(vert_index % 2 == 0, lower, sz.nv - 1 - lower), sz.nv)


def beam_weights(speed):
    s = jnp.abs(speed) * time_increment
    return -1.5 * s + 0.5 * s * s, 2.0 * s - s * s, -0.5 * s + 0.5 * s * s


class Edges:
    def __init__(self, sz, parity):
        cells = sz.cells
        y = lanes(sz) % Y
        y = jnp.broadcast_to(y, (SUB, cells))
        even = parity == 0
        self.pair = y // 2
        self.odd_lane = y % 2
        first = jnp.where(even, 0, Y - 1)
        second = jnp.where(even, 1, Y - 2)
        self.one = y == first
        self.two = self.one | (y == second)
        self.shift_one = jnp.where(even, cells - 1, 1)
        self.shift_two = jnp.where(even, cells - 2, 2)
        self.unpack = jnp.where(even, Y, cells - 2)
        self.pack = jnp.where(even, 0, cells - (Y - 2))
        self.cells = cells

    def unpack_shift(self, slot):
        return lax.rem(self.unpack + (self.cells - 2 * slot), self.cells)

    def pack_shift(self, slot):
        return lax.rem(self.pack + 2 * slot, self.cells)


def roll(value, shift):
    if isinstance(shift, int) and shift == 0:
        return value
    return pltpu.roll(value, shift, 1)


class Packer:
    def __init__(self, sz, edges, right):
        self.sz, self.edges, self.right = sz, edges, right
        self.wall = self.side = None
        lane = lax.broadcasted_iota(jnp.int32, (SUB, sz.cells), 1)
        self.side_slot = lane // (2 * Y)

    def add(self, value, k):
        sz = self.sz
        slot = k % SUB
        moved = roll(value, self.edges.pack_shift(slot))
        self.wall = moved if slot == 0 else jnp.where(self.edges.pair == slot, moved, self.wall)
        slot = k % sz.side_slots
        shift = 2 * Y * slot
        if self.right:
            shift = (shift + 2 * Y) % sz.cells
        moved = roll(value, shift % sz.cells)
        self.side = moved if slot == 0 else jnp.where(self.side_slot == slot, moved, self.side)


def put_moments(sz, vert_index, sums, packet_ref, mirror_ref):
    (n, mx, my, pxx, pxy, pyy, extra, tx, ty) = [
        jnp.sum(part, axis=0, keepdims=True) * sz.weight for part in sums
    ]
    even = vert_index % 2 == 0
    zero = jnp.zeros_like(n)
    rows = [n, mx, my, pxx + pyy + extra, pxx, pxy, pyy, tx, ty]
    rows += [jnp.where(even, -my, zero), jnp.where(even, zero, my)]
    rows += [zero] * (ROWS - len(rows))
    for r, row in enumerate(rows):
        packet_ref[r : r + 1, :] = row
        mirror_ref[sz.mirror_blocks + r // SUB, r % SUB : r % SUB + 1, :] = row


class Moments:
    def __init__(self, shape):
        zero = jnp.zeros(shape, jnp.float32)
        self.g = [zero] * 4
        self.h = [zero] * 2

    def add(self, g, h):
        for sums, item in ((self.g, g), (self.h, h)):
            for order in range(len(sums)):
                item = sums[order] + item
                sums[order] = item

    def finish(self, sz, vert_index, speed_x, totals):
        s0, s1, s2, s3 = self.g
        m1, m2, m3 = s1, 2.0 * s2 - s1, 6.0 * (s3 - s2) + s1
        first = row_speed(sz, vert_index, jnp.zeros((1, 1), jnp.int32))
        last = row_speed(sz, vert_index, jnp.full((1, 1), sz.band, jnp.int32))
        b = jnp.broadcast_to(last, s0.shape)
        d = (last - first) / sz.band
        d = jnp.broadcast_to(d, s0.shape)
        t0 = s0
        t1 = b * s0 - d * m1
        t2 = b * (b * s0 - 2.0 * d * m1) + d * d * m2
        t3 = b * (b * (b * s0 - 3.0 * d * m1) + 3.0 * d * d * m2) - d * d * d * m3
        u0, su1 = self.h
        u1 = b * u0 - d * su1
        x2 = speed_x * speed_x
        new = (
            t0,
            speed_x * t0,
            t1,
            x2 * t0,
            speed_x * t1,
            t2,
            u0,
            speed_x * (x2 * t0 + t2 + u0),
            x2 * t1 + t3 + u1,
        )
        return tuple(a + c for a, c in zip(totals, new))


def zero_totals(sz):
    return tuple(jnp.zeros((SUB, sz.cells), jnp.float32) for _ in range(9))


def wall_rows(sz, face, type_ref, index_ref, temps_ref, acc_ref, wall_ref):
    lane = lanes(sz)
    column = lane // Y
    kind = jnp.zeros_like(lane)
    entry = jnp.zeros_like(lane)
    for x in range(sz.cells // Y):
        kind = jnp.where(column == x, type_ref[face, x], kind)
        entry = jnp.where(column == x, index_ref[face, x], entry)
    percent = jnp.zeros_like(lane)
    for t in range(NTYPE):
        percent = jnp.where(kind == t, acc_ref[t], percent)
    alpha = percent.astype(jnp.float32) / 100.0
    heat = jnp.ones((1, sz.cells), jnp.float32)
    denom = jnp.ones((1, sz.cells), jnp.float32)

    def grid(number):
        index = lax.broadcasted_iota(jnp.int32, (1, -(-number // 128) * 128), 1)
        return node_speed(index, number), index < number

    vx, in_x = grid(sz.nx)
    vy, in_y = grid(sz.nv)
    for t in range(NTEMP):
        temp = jnp.full((1, 1), temps_ref[t], jnp.float32)
        along = jnp.sum(jnp.where(in_x, jnp.exp(-vx * vx / temp), 0.0), axis=1, keepdims=True)
        across = jnp.sum(
            jnp.where(in_y, jnp.maximum(vy, 0.0) * jnp.exp(-vy * vy / temp), 0.0),
            axis=1,
            keepdims=True,
        )
        inward = sz.weight * along * across / (math.pi * temp)
        heat = jnp.where(entry == t, temp, heat)
        denom = jnp.where(entry == t, inward, denom)
    wall_ref[0:1, :] = alpha / (denom * (math.pi * heat))
    wall_ref[1:2, :] = 1.0 - alpha
    wall_ref[2:3, :] = heat
    wall_ref[3:SUB, :] = jnp.zeros((SUB - 3, sz.cells), jnp.float32)


def group_speed(sz, group):
    index = lax.broadcasted_iota(jnp.int32, (SUB, sz.cells), 0) + group * SUB
    return node_speed(index, sz.nx)


def first_kernel(sz, state, type_ref, index_ref, temps_ref, acc_ref, mirror, packet, right, left, wall):
    vert_index = lax.axis_index("vert")
    parity = vert_index % 2
    edges = Edges(sz, parity)
    wall_rows(sz, 1 - parity, type_ref, index_ref, temps_ref, acc_ref, wall)
    totals = zero_totals(sz)
    for positive in (False, True):
        out = right if positive else left

        def group_body(local, totals):
            group = local + (sz.half if positive else 0)
            rows = pl.ds(pl.multiple_of(group * SUB, SUB), SUB)
            sums = Moments((SUB, sz.cells))
            packers = [Packer(sz, edges, positive) for _ in range(2)]
            for k in range(sz.band):
                values = [state[f, k, rows, :] for f in range(2)]
                sums.add(*values)
                send_rows(sz, packers, values, k, local, group, mirror, out)
            return sums.finish(sz, vert_index, group_speed(sz, group), totals)

        totals = lax.fori_loop(0, sz.half, group_body, totals)
    put_moments(sz, vert_index, totals, packet, mirror)


def send_rows(sz, packers, values, k, local, group, mirror, side):
    for f in range(2):
        packers[f].add(values[f], k)
        if k % SUB == SUB - 1 or k == sz.band - 1:
            mirror[sz.mirror_index(f, group, k // SUB)] = packers[f].wall
        if k % sz.side_slots == sz.side_slots - 1 or k == sz.band - 1:
            side[f, local, k // sz.side_slots] = packers[f].side


def step_kernel(sz, last, *refs):
    refs = list(refs)
    state, mirror_in, right_in, left_in, packet_in, wall = refs[:6]
    others = refs[6 : 6 + sz.vert - 2]
    rest = refs[6 + sz.vert - 2 :]
    if last:
        (out, ey_ref, py_ref, cy_ref, c0_ref, y1_ref, y2_ref) = rest
    else:
        (out, mirror, packet, right, left, ey_ref, py_ref, cy_ref, c0_ref, y1_ref, y2_ref) = rest
    cells = sz.cells
    vert_index = lax.axis_index("vert")
    parity = vert_index % 2
    edges = Edges(sz, parity)
    even = parity == 0
    lane8 = lax.broadcasted_iota(jnp.int32, (SUB, cells), 1)

    blocks = sz.mirror_blocks
    tot = [packet_in[SUB * b : SUB * b + SUB, :] + mirror_in[blocks + b] for b in range(2)]
    for other in others:
        tot = [tot[b] + other[SUB * b : SUB * b + SUB, :] for b in range(2)]

    def row(r):
        return tot[r // SUB][r % SUB : r % SUB + 1, :]

    n, mx, my, energy, pxx, pxy, pyy, tx, ty = [row(r) for r in range(9)]
    inv_n = 1.0 / n
    ux, uy = mx * inv_n, my * inv_n
    usq = ux * ux + uy * uy
    theta = 2.0 / 3.0 * (energy * inv_n - usq)
    along = ux * mx + uy * my
    qx = tx - 2.0 * (ux * pxx + uy * pxy) + usq * mx - ux * energy + 2.0 * ux * along - ux * usq * n
    qy = ty - 2.0 * (ux * pxy + uy * pyy) + usq * my - uy * energy + 2.0 * uy * along - uy * usq * n
    inv_t = 1.0 / theta
    rate = (time_increment * relaxation_multiplier) * n * jnp.exp(shear_exponent * jnp.log(theta))
    amount = rate * n * inv_t * (1.0 / math.pi)
    flux_scale = (1.0 - diffusivity_ratio) * 0.8 * inv_n * inv_t * inv_t
    half_theta = jnp.broadcast_to(0.5 * theta, (SUB, cells))
    px, py = flux_scale * qx, flux_scale * qy

    vy = row_speed(sz, vert_index, lax.broadcasted_iota(jnp.int32, (sz.band, cells), 0))
    cy = vy - uy
    cy_sq = cy * cy * inv_t
    ey_ref[...] = amount * jnp.exp(-cy_sq)
    py_ref[...] = py * cy
    cy_ref[...] = cy_sq - 2.0
    b0, b1, b2 = beam_weights(vy)
    c0_ref[...] = (1.0 + b0) - rate
    y1_ref[...] = b1
    y2_ref[...] = b2

    y = lanes(sz) % Y
    flux = jnp.where(even, row(10), row(9))
    flux = jnp.where(y == jnp.where(even, Y - 1, 0), flux, 0.0)
    for span in (1, 2, 4, 8):
        flux = flux + roll(flux, jnp.where(even, cells - span, span))
    heat = wall[2:3, :]
    inv_heat = 1.0 / heat
    half_heat = jnp.broadcast_to(0.5 * heat, (SUB, cells))
    keep = jnp.broadcast_to(wall[1:2, :], (SUB, cells))
    emitted = flux * wall[0:1, :]
    wall_y = []
    for pack in range(sz.wall_packs):
        speed = row_speed(sz, vert_index, pack * SUB + y // 2)
        wall_y.append(jnp.broadcast_to(emitted * jnp.exp(-speed * speed * inv_heat), (SUB, cells)))

    totals = zero_totals(sz)
    for positive in (False, True):
        side_in = right_in if positive else left_in
        side_out = None if last else (right if positive else left)
        if positive:
            x_one, x_two = lane8 >= cells - Y, lane8 >= cells - 2 * Y
            x_shift = (Y, 2 * Y)
        else:
            x_one, x_two = lane8 < Y, lane8 < 2 * Y
            x_shift = (cells - Y, cells - 2 * Y)

        def group_body(local, totals):
            group = local + (sz.half if positive else 0)
            rows = pl.ds(pl.multiple_of(group * SUB, SUB), SUB)
            vx = group_speed(sz, group)
            cx = vx - ux
            cx_sq = cx * cx * inv_t
            ex = jnp.exp(-cx_sq)
            pxs = px * cx
            x0, x1, x2 = beam_weights(vx)
            wall_x = jnp.exp(-vx * vx * inv_heat)
            sums = Moments((SUB, cells))
            packers = [Packer(sz, edges, positive) for _ in range(2)]
            ghosts = sides = None
            for k in range(sz.band):
                slot = k % SUB
                if slot == 0:
                    diffuse = wall_x * wall_y[k // SUB]
                    ghosts = []
                    for f in range(2):
                        got = mirror_in[sz.mirror_index(f, group, k // SUB)]
                        got = jnp.where(edges.odd_lane == 1, roll(got, 1), roll(got, cells - 1))
                        ghosts.append(keep * got + (half_heat * diffuse if f else diffuse))
                side_slot = k % sz.side_slots
                if side_slot == 0:
                    sides = [side_in[f, local, k // sz.side_slots] for f in range(2)]
                shift = -2 * Y * side_slot
                if positive:
                    shift -= 2 * Y
                shift = shift % cells
                at = pl.ds(k, 1)
                maxwell = ex * ey_ref[at, :]
                p = pxs + py_ref[at, :]
                c2 = cx_sq + cy_ref[at, :]
                sg = maxwell * (1.0 + p * c2)
                sh = half_theta * (sg + p * maxwell)
                c0 = x0 + c0_ref[at, :]
                y1, y2 = y1_ref[at, :], y2_ref[at, :]
                values = []
                for f, source in ((0, sg), (1, sh)):
                    v = state[f, k, rows, :]
                    ghost = roll(ghosts[f], edges.unpack_shift(slot))
                    side = roll(sides[f], shift)
                    moved = v * c0 + source
                    moved = moved + x1 * roll(jnp.where(x_one, side, v), x_shift[0])
                    moved = moved + x2 * roll(jnp.where(x_two, side, v), x_shift[1])
                    moved = moved + y1 * roll(jnp.where(edges.one, ghost, v), edges.shift_one)
                    moved = moved + y2 * roll(jnp.where(edges.two, ghost, v), edges.shift_two)
                    out[f, k, rows, :] = moved
                    values.append(moved)
                if not last:
                    sums.add(*values)
                    send_rows(sz, packers, values, k, local, group, mirror, side_out)
            if last:
                return totals
            return sums.finish(sz, vert_index, vx, totals)

        totals = lax.fori_loop(0, sz.half, group_body, () if last else totals)
        totals = zero_totals(sz) if last else totals
    if not last:
        put_moments(sz, vert_index, totals, packet, mirror)


def shapes(sz):
    f32 = jnp.float32
    side = jax.ShapeDtypeStruct((2, sz.half, sz.side_packs, SUB, sz.cells), f32)
    return (
        jax.ShapeDtypeStruct((sz.mirror_blocks + 2, SUB, sz.cells), f32),
        jax.ShapeDtypeStruct((ROWS, sz.cells), f32),
        side,
        side,
    )


def on_device(distribution, wall_type, wall_temp_index, wall_temps, accommodation):
    _, band, nx, cells = distribution.shape
    vert = lax.axis_size("vert")
    columns = lax.axis_size("gx")
    sz = Sizes(band, nx, cells, vert)
    vmem = pl.BlockSpec(memory_space=pltpu.VMEM)
    smem = pl.BlockSpec(memory_space=pltpu.SMEM)
    state_shape = jax.ShapeDtypeStruct(distribution.shape, jnp.float32)
    bytes_moved = 2 * distribution.size * 4
    state = distribution
    mirror, packet, right, left, wall = pl.pallas_call(
        functools.partial(first_kernel, sz),
        out_shape=shapes(sz) + (jax.ShapeDtypeStruct((SUB, cells), jnp.float32),),
        in_specs=[vmem] + [smem] * 4,
        out_specs=(vmem,) * 5,
        cost_estimate=pl.CostEstimate(
            flops=10 * state.size, bytes_accessed=bytes_moved // 2, transcendentals=0
        ),
        name="first",
    )(state, wall_type, wall_temp_index, wall_temps, accommodation)
    ring = [(i, (i + 1) % columns) for i in range(columns)]
    back = [(j, i) for i, j in ring]
    for iteration in range(ITERS):
        last = iteration == ITERS - 1
        mirror_in = lax.ppermute(mirror, "vert", [(s, s ^ 1) for s in range(vert)])
        right_in = lax.ppermute(right, "gx", ring)
        left_in = lax.ppermute(left, "gx", back)
        others = []
        for mask in range(vert - 1, 1, -1):
            others.append(lax.ppermute(packet, "vert", [(s, s ^ mask) for s in range(vert)]))
        result = pl.pallas_call(
            functools.partial(step_kernel, sz, last),
            out_shape=(state_shape,) if last else (state_shape,) + shapes(sz),
            in_specs=[vmem] * (6 + len(others)),
            out_specs=(vmem,) if last else (vmem,) * 5,
            scratch_shapes=[pltpu.VMEM((band, cells), jnp.float32)] * 6,
            cost_estimate=pl.CostEstimate(
                flops=40 * state.size, bytes_accessed=bytes_moved, transcendentals=0
            ),
            name="last" if last else "step",
        )(state, mirror_in, right_in, left_in, packet, wall, *others)
        if last:
            (state,) = result
        else:
            state, mirror, packet, right, left = result
    return state


def solution(mesh):
    placed = (P(None, "vert", None, "gx"), P(None, "gx"), P(None, "gx"), P(), P())
    return jax.shard_map(
        on_device,
        mesh=mesh,
        in_specs=placed,
        out_specs=P(None, "vert", None, "gx"),
        check_vma=False,
    )
```

time: 594 us -> 158 us (0.27); the launches traced: 583 us -> 158 us
  local copies, waits for them, and re-layouts: 396 us -> 3.59 us
  other arithmetic: 112 us -> 0 us
  Pallas kernels: 0 us -> 108 us
  blocking collectives: 38.2 us -> 0 us
  starting transfers between devices: 11.5 us -> 29.4 us
  matrix products: 11.4 us -> 0 us
    slice x70 -> x0, local copies, waits for them, and re-layouts: 284 us -> none  [the longest x16 99.7 us: on_device(): bottom_rows = jnp.stack([state[..., 0::Y], state[..., 1::Y]])]
    pallas_call x0 -> x5, Pallas kernels: none -> 108 us  [the longest x4 103 us: on_device(): pl.pallas_call(functools.partial(step_kernel, sz, last), out_shape=(state...]
    add x8 -> x0, other arithmetic: 66.7 us -> none  [the longest x4 62 us: advance(): return moved + relaxation_frequency * (target - state)]
    reshape x16 -> x0, local copies, waits for them, and re-layouts: 40.6 us -> none  [spread(): return jnp.repeat(ghost, Y, axis=-1)]
    psum x4 -> x0, blocking collectives: 38.2 us -> none  [on_device(): lax.psum((raw_moments(state, speed_x, speed_y), flux_part), 'vert')]
    ppermute x8 -> x0, local copies, waits for them, and re-layouts: 26.2 us -> none  [the longest x4 13.3 us: with_halo(): lax.ppermute(head, axis, [((i + 1) % count, i) for i in range(count)])]
    mul x34 -> x0, other arithmetic: 21.5 us -> none  [the longest x4 10.7 us: shakhov_target(): relaxed_distribution_target * (1.0 + multiplier_coefficient * (kinetic_co...]
    ppermute x12 -> x20, starting transfers between devices: 11.5 us -> 29.4 us  [the longest x8 13.8 us: on_device(): lax.ppermute(packet, 'vert', [(s, s ^ mask) for s in range(vert)])]
  transfers between devices with their start and end apart: 12 -> 20, of which waited for: 2 -> 9; matrix products, arithmetic and copies ran while one was open for 29% -> 0% of each run, Pallas kernels for 0% -> 0%
where the time goes in v1:
time: 158 us
  Pallas kernels  108 us (68%)
  starting transfers between devices  29.4 us (19%)
  waiting for transfers between devices  17 us (11%)
  local copies, waits for them, and re-layouts  3.59 us (2%)
    pallas_call x4, Pallas kernels, on_device(): pl.pallas_call(functools.partial(step_kernel, sz, last), out_shape=(state...  103 us
    ppermute x8, waiting for transfers between devices, on_device(): lax.ppermute(packet, 'vert', [(s, s ^ mask) for s in range(vert)])  16.6 us
    ppermute x8, starting transfers between devices, on_device(): lax.ppermute(packet, 'vert', [(s, s ^ mask) for s in range(vert)])  13.8 us
    ppermute x4, starting transfers between devices, on_device(): left_in = lax.ppermute(left, 'gx', back)  9.84 us
    ppermute x4, starting transfers between devices, on_device(): mirror_in = lax.ppermute(mirror, 'vert', [(s, s ^ 1) for s in range(vert)])  4.89 us
    pallas_call x1, Pallas kernels, on_device(): pl.pallas_call(functools.partial(first_kernel, sz), out_shape=shapes(sz)...  4.51 us
    unnamed x40, local copies, waits for them, and re-layouts  3.59 us
  transfers between devices with their start and end apart: 20, of which 9 were waited for; matrix products, arithmetic and copies ran while one was open for 0% of the time, Pallas kernels for 0%

profile of v1, /device:TPU:0, one launch (start us, length us, event | category | flops | bytes accessed | tf_op | source)
XLA Modules:
  0.0 158.0 jit_solution(14986322872704898267)
XLA Ops:
  0.0 4.5 %first.1 = (f32[74,8,128]{2,1,0:T(8,128)}, f32[16,128]{1,0:T(8,128)}, f32[2,6,6,8,128]{4,3,2,1,0:T(8,128)}, f32[2,6,6,8,128]{4,3,2,1,0:T(8,128)}, f32[8,128]{1,0:T(8,128)}) custom-call(f32[2,24,96,128]{3,2,1,0:T(8,128)} %refs_0_.1, s32[2,8]{1,0:T(2,128)} %type_ref.1, s32[2,8]{1,0:T(2,128)} %index_ref.1, f32[2]{0:T(128)} %temps_ref.1, s32[3]{0:T(128)} %acc_ref.1), custom_call_target="tpu_custom_call" | custom-call | flops 5898240 | bytes 2359296 | tf_op jit(solution)/shard_map/first/pallas_call | solution.py:409
  4.5 3.1 %collective-permute-start = (f32[74,8,128]{2,1,0:T(8,128)}, f32[74,8,128]{2,1,0:T(8,128)S(1)}, u32[]{:S(2)}, u32[]{:S(2)}) collective-permute-start(f32[74,8,128]{2,1,0:T(8,128)} %get-tuple-element.25), channel_id=1, source_target_pairs={{0,1},{1,0},{2,3},{3,2},{4,5},{5,4},{6,7},{7,6},{8,9},{9,8},{10,11... | collective-permute-start | bytes 909320 | tf_op jit(solution)/shard_map/ppermute | solution.py:423
  7.6 0.0 collective-permute-start.1
  7.6 2.6 %collective-permute-start.2 = (f32[2,6,6,8,128]{4,3,2,1,0:T(8,128)}, f32[2,6,6,8,128]{4,3,2,1,0:T(8,128)S(1)}, u32[]{:S(2)}, u32[]{:S(2)}) collective-permute-start(f32[2,6,6,8,128]{4,3,2,1,0:T(8,128)} %get-tuple-element.27), channel_id=1, source_target_pairs={{4,0},{8,4},{12,8},{16,12},{20,16},{24,20},{28,24},{0,28},{5,1},{9... | collective-permute-start | bytes 884744 | tf_op jit(solution)/shard_map/ppermute | solution.py:425
  10.2 2.6 %collective-permute-start.4 = (f32[16,128]{1,0:T(8,128)}, f32[16,128]{1,0:T(8,128)S(1)}, u32[]{:S(2)}, u32[]{:S(2)}) collective-permute-start(f32[16,128]{1,0:T(8,128)} %get-tuple-element.28.refs_4_), channel_id=1, source_target_pairs={{0,2},{1,3},{2,0},{3,1},{4,6},{5,7},{6,4},{7,5},{8,10},{9,11},{10,... | collective-permute-start | bytes 24584 | tf_op jit(solution)/shard_map/ppermute | solution.py:428
  12.8 0.0 collective-permute-start.3
  12.8 2.3 %collective-permute-done.4.refs_7_ = f32[16,128]{1,0:T(8,128)S(1)} collective-permute-done((f32[16,128]{1,0:T(8,128)}, f32[16,128]{1,0:T(8,128)S(1)}, u32[]{:S(2)}, u32[]{:S(2)}) %collective-permute-start.4) | collective-permute-done | bytes 8224 | tf_op jit(solution)/shard_map/ppermute | solution.py:428
  15.1 3.4 %collective-permute-done.3.refs_6_ = f32[16,128]{1,0:T(8,128)S(1)} collective-permute-done((f32[16,128]{1,0:T(8,128)}, f32[16,128]{1,0:T(8,128)S(1)}, u32[]{:S(2)}, u32[]{:S(2)}) %collective-permute-start.3) | collective-permute-done | bytes 8224 | tf_op jit(solution)/shard_map/ppermute | solution.py:428
  18.5 0.0 collective-permute-done.1.refs_2_
  18.5 0.0 collective-permute-done.2.refs_3_
  18.5 0.0 copy-start.9
  18.5 0.0 collective-permute-done.refs_1_
  18.5 0.5 copy-done.17
  19.1 0.1 copy-done.6
  19.2 0.1 copy-done.9
  19.3 0.1 copy-done.3
  19.4 26.7 %step.3 = (f32[2,24,96,128]{3,2,1,0:T(8,128)}, f32[74,8,128]{2,1,0:T(8,128)}, f32[16,128]{1,0:T(8,128)}, f32[2,6,6,8,128]{4,3,2,1,0:T(8,128)}, f32[2,6,6,8,128]{4,3,2,1,0:T(8,128)}) custom-call(f32[2,24,96,128]{3,2,1,0:T(8,128)} %refs_0_.1, f32[74,8,128]{2,1,0:T(8,128)} %copy-done.3, f32[2,6,6,8,128]{4,3,2,1,0:T(8,128)} %copy-done.6, ...), custom_call_target="tpu_custom_call" | custom-call | flops 23592960 | bytes 4718592 | tf_op jit(solution)/shard_map/step/pallas_call | solution.py:429
  46.1 0.0 collective-permute-start.5
  46.1 0.1 collective-permute-start.6
  46.1 2.6 %collective-permute-start.7 = (f32[2,6,6,8,128]{4,3,2,1,0:T(8,128)}, f32[2,6,6,8,128]{4,3,2,1,0:T(8,128)S(1)}, u32[]{:S(2)}, u32[]{:S(2)}) collective-permute-start(f32[2,6,6,8,128]{4,3,2,1,0:T(8,128)} %get-tuple-element.33), channel_id=1, source_target_pairs={{4,0},{8,4},{12,8},{16,12},{20,16},{24,20},{28,24},{0,28},{5,1},{9... | collective-permute-start | bytes 884744 | tf_op jit(solution)/shard_map/ppermute | solution.py:425
  48.8 1.0 collective-permute-start.9
  49.8 3.3 %collective-permute-start.8 = (f32[16,128]{1,0:T(8,128)}, f32[16,128]{1,0:T(8,128)S(1)}, u32[]{:S(2)}, u32[]{:S(2)}) collective-permute-start(f32[16,128]{1,0:T(8,128)} %get-tuple-element.34.refs_4_), channel_id=1, source_target_pairs={{0,3},{1,2},{2,1},{3,0},{4,7},{5,6},{6,5},{7,4},{8,11},{9,10},{10,... | collective-permute-start | bytes 24584 | tf_op jit(solution)/shard_map/ppermute | solution.py:428
  53.1 0.5 collective-permute-done.9.refs_7_
  53.6 2.1 %collective-permute-done.8.refs_6_ = f32[16,128]{1,0:T(8,128)S(1)} collective-permute-done((f32[16,128]{1,0:T(8,128)}, f32[16,128]{1,0:T(8,128)S(1)}, u32[]{:S(2)}, u32[]{:S(2)}) %collective-permute-start.8) | collective-permute-done | bytes 8224 | tf_op jit(solution)/shard_map/ppermute | solution.py:428
  55.7 0.0 collective-permute-done.6.refs_2_
  55.7 0.0 collective-permute-done.7.refs_3_
  55.7 0.0 copy-start.7
  55.7 0.0 collective-permute-done.5.refs_1_
  55.8 0.5 copy-done.15
  56.3 0.1 copy-done.4
  56.4 0.1 copy-done.7
  56.6 0.1 copy-done.1
  56.6 26.6 %step.4 = (f32[2,24,96,128]{3,2,1,0:T(8,128)}, f32[74,8,128]{2,1,0:T(8,128)}, f32[16,128]{1,0:T(8,128)}, f32[2,6,6,8,128]{4,3,2,1,0:T(8,128)}, f32[2,6,6,8,128]{4,3,2,1,0:T(8,128)}) custom-call(f32[2,24,96,128]{3,2,1,0:T(8,128)} %get-tuple-element.30.refs_0_, f32[74,8,128]{2,1,0:T(8,128)} %copy-done.1, f32[2,6,6,8,128]{4,3,2,1,0:T(8,128)} %copy-done.4, ...), custom_call_target="tpu_custom_call" | custom-call | flops 23592960 | bytes 4718592 | tf_op jit(solution)/shard_map/step/pallas_call | solution.py:429
  83.3 1.8 %collective-permute-start.10 = (f32[74,8,128]{2,1,0:T(8,128)}, f32[74,8,128]{2,1,0:T(8,128)S(1)}, u32[]{:S(2)}, u32[]{:S(2)}) collective-permute-start(f32[74,8,128]{2,1,0:T(8,128)} %get-tuple-element.36), channel_id=1, source_target_pairs={{0,1},{1,0},{2,3},{3,2},{4,5},{5,4},{6,7},{7,6},{8,9},{9,8},{10,11... | collective-permute-start | bytes 909320 | tf_op jit(solution)/shard_map/ppermute | solution.py:423
  85.1 0.3 collective-permute-start.11
  85.4 2.4 %collective-permute-start.12 = (f32[2,6,6,8,128]{4,3,2,1,0:T(8,128)}, f32[2,6,6,8,128]{4,3,2,1,0:T(8,128)S(1)}, u32[]{:S(2)}, u32[]{:S(2)}) collective-permute-start(f32[2,6,6,8,128]{4,3,2,1,0:T(8,128)} %get-tuple-element.38), channel_id=1, source_target_pairs={{4,0},{8,4},{12,8},{16,12},{20,16},{24,20},{28,24},{0,28},{5,1},{9... | collective-permute-start | bytes 884744 | tf_op jit(solution)/shard_map/ppermute | solution.py:425
  87.7 1.8 %collective-permute-start.14 = (f32[16,128]{1,0:T(8,128)}, f32[16,128]{1,0:T(8,128)S(1)}, u32[]{:S(2)}, u32[]{:S(2)}) collective-permute-start(f32[16,128]{1,0:T(8,128)} %get-tuple-element.39.refs_4_), channel_id=1, source_target_pairs={{0,2},{1,3},{2,0},{3,1},{4,6},{5,7},{6,4},{7,5},{8,10},{9,11},{10,... | collective-permute-start | bytes 24584 | tf_op jit(solution)/shard_map/ppermute | solution.py:428
  89.5 0.8 collective-permute-start.13
  90.3 2.5 %collective-permute-done.14.refs_7_ = f32[16,128]{1,0:T(8,128)S(1)} collective-permute-done((f32[16,128]{1,0:T(8,128)}, f32[16,128]{1,0:T(8,128)S(1)}, u32[]{:S(2)}, u32[]{:S(2)}) %collective-permute-start.14) | collective-permute-done | bytes 8224 | tf_op jit(solution)/shard_map/ppermute | solution.py:428
  92.8 2.4 %collective-permute-done.13.refs_6_ = f32[16,128]{1,0:T(8,128)S(1)} collective-permute-done((f32[16,128]{1,0:T(8,128)}, f32[16,128]{1,0:T(8,128)S(1)}, u32[]{:S(2)}, u32[]{:S(2)}) %collective-permute-start.13) | collective-permute-done | bytes 8224 | tf_op jit(solution)/shard_map/ppermute | solution.py:428
  95.2 0.3 collective-permute-done.11.refs_2_
  95.5 0.0 collective-permute-done.12.refs_3_
  95.5 0.0 collective-permute-done.10.refs_1_
  95.5 0.0 copy-start.2
  95.5 0.3 copy-done.16
  95.8 0.4 copy-done.5
  96.2 0.1 copy-done.8
  96.3 0.1 copy-done.2
  96.4 26.7 %step.5 = (f32[2,24,96,128]{3,2,1,0:T(8,128)}, f32[74,8,128]{2,1,0:T(8,128)}, f32[16,128]{1,0:T(8,128)}, f32[2,6,6,8,128]{4,3,2,1,0:T(8,128)}, f32[2,6,6,8,128]{4,3,2,1,0:T(8,128)}) custom-call(f32[2,24,96,128]{3,2,1,0:T(8,128)} %get-tuple-element.35.refs_0_, f32[74,8,128]{2,1,0:T(8,128)} %copy-done.2, f32[2,6,6,8,128]{4,3,2,1,0:T(8,128)} %copy-done.5, ...), custom_call_target="tpu_custom_call" | custom-call | flops 23592960 | bytes 4718592 | tf_op jit(solution)/shard_map/step/pallas_call | solution.py:429
  123.1 0.0 collective-permute-start.15
  123.1 0.5 collective-permute-start.16
  123.6 2.2 %collective-permute-start.17 = (f32[2,6,6,8,128]{4,3,2,1,0:T(8,128)}, f32[2,6,6,8,128]{4,3,2,1,0:T(8,128)S(1)}, u32[]{:S(2)}, u32[]{:S(2)}) collective-permute-start(f32[2,6,6,8,128]{4,3,2,1,0:T(8,128)} %get-tuple-element.43), channel_id=1, source_target_pairs={{4,0},{8,4},{12,8},{16,12},{20,16},{24,20},{28,24},{0,28},{5,1},{9... | collective-permute-start | bytes 884744 | tf_op jit(solution)/shard_map/ppermute | solution.py:425
  125.8 2.2 %collective-permute-start.19 = (f32[16,128]{1,0:T(8,128)}, f32[16,128]{1,0:T(8,128)S(1)}, u32[]{:S(2)}, u32[]{:S(2)}) collective-permute-start(f32[16,128]{1,0:T(8,128)} %get-tuple-element.44.refs_4_), channel_id=1, source_target_pairs={{0,2},{1,3},{2,0},{3,1},{4,6},{5,7},{6,4},{7,5},{8,10},{9,11},{10,... | collective-permute-start | bytes 24584 | tf_op jit(solution)/shard_map/ppermute | solution.py:428
  128.0 2.2 %collective-permute-start.18 = (f32[16,128]{1,0:T(8,128)}, f32[16,128]{1,0:T(8,128)S(1)}, u32[]{:S(2)}, u32[]{:S(2)}) collective-permute-start(f32[16,128]{1,0:T(8,128)} %get-tuple-element.44.refs_4_), channel_id=1, source_target_pairs={{0,3},{1,2},{2,1},{3,0},{4,7},{5,6},{6,5},{7,4},{8,11},{9,10},{10,... | collective-permute-start | bytes 24584 | tf_op jit(solution)/shard_map/ppermute | solution.py:428
  130.1 0.8 collective-permute-done.19.refs_7_
  131.0 2.7 %collective-permute-done.18.refs_6_ = f32[16,128]{1,0:T(8,128)S(1)} collective-permute-done((f32[16,128]{1,0:T(8,128)}, f32[16,128]{1,0:T(8,128)S(1)}, u32[]{:S(2)}, u32[]{:S(2)}) %collective-permute-start.18) | collective-permute-done | bytes 8224 | tf_op jit(solution)/shard_map/ppermute | solution.py:428
  133.6 0.0 collective-permute-done.16.refs_2_
  133.6 0.0 collective-permute-done.17.refs_3_
  133.7 0.0 collective-permute-done.15.refs_1_
  133.7 0.5 copy-done.19
  134.2 0.1 copy-done.10
  134.4 0.1 copy-done.11
  134.5 0.1 copy-done
  134.6 23.4 %last.1 = f32[2,24,96,128]{3,2,1,0:T(8,128)} custom-call(f32[2,24,96,128]{3,2,1,0:T(8,128)} %get-tuple-element.40.refs_0_, f32[74,8,128]{2,1,0:T(8,128)} %copy-done, f32[2,6,6,8,128]{4,3,2,1,0:T(8,128)} %copy-done.10, f32[2,6,6,8,128]{4,3,2,1,0:T(8,128)} %copy-done.11, f32[16,128]{1,0:T(8,128)} %get-tuple-element.44.refs_4_, ...), custom_call_target="tpu_custom_call" | custom-call | flops 23592960 | bytes 4718592 | tf_op jit(solution)/shard_map/last/pallas_call | solution.py:429
  (21 shorter events, 0.0 us)
Async XLA Ops:
  4.5 14.0 %collective-permute-start = (f32[74,8,128]{2,1,0:T(8,128)}, f32[74,8,128]{2,1,0:T(8,128)S(1)}, u32[]{:S(2)}, u32[]{:S(2)}) collective-permute-start(f32[74,8,128]{2,1,0:T(8,128)} %get-tuple-element.25), channel_id=1, source_target_pairs={{0,1},{1,0},{2,3},{3,2},{4,5},{5,4},{6,7},{7,6},{8,9},{9,8},{10,11... | collective-permute-start | bytes 909320 | tf_op jit(solution)/shard_map/ppermute | solution.py:423
  7.6 10.9 %collective-permute-start.1 = (f32[2,6,6,8,128]{4,3,2,1,0:T(8,128)}, f32[2,6,6,8,128]{4,3,2,1,0:T(8,128)S(1)}, u32[]{:S(2)}, u32[]{:S(2)}) collective-permute-start(f32[2,6,6,8,128]{4,3,2,1,0:T(8,128)} %get-tuple-element.26), channel_id=1, source_target_pairs={{0,4},{4,8},{8,12},{12,16},{16,20},{20,24},{24,28},{28,0},{1,5},{5... | collective-permute-start | bytes 884744 | tf_op jit(solution)/shard_map/ppermute | solution.py:424
  7.6 10.9 %collective-permute-start.2 = (f32[2,6,6,8,128]{4,3,2,1,0:T(8,128)}, f32[2,6,6,8,128]{4,3,2,1,0:T(8,128)S(1)}, u32[]{:S(2)}, u32[]{:S(2)}) collective-permute-start(f32[2,6,6,8,128]{4,3,2,1,0:T(8,128)} %get-tuple-element.27), channel_id=1, source_target_pairs={{4,0},{8,4},{12,8},{16,12},{20,16},{24,20},{28,24},{0,28},{5,1},{9... | collective-permute-start | bytes 884744 | tf_op jit(solution)/shard_map/ppermute | solution.py:425
  10.2 4.9 %collective-permute-start.4 = (f32[16,128]{1,0:T(8,128)}, f32[16,128]{1,0:T(8,128)S(1)}, u32[]{:S(2)}, u32[]{:S(2)}) collective-permute-start(f32[16,128]{1,0:T(8,128)} %get-tuple-element.28.refs_4_), channel_id=1, source_target_pairs={{0,2},{1,3},{2,0},{3,1},{4,6},{5,7},{6,4},{7,5},{8,10},{9,11},{10,... | collective-permute-start | bytes 24584 | tf_op jit(solution)/shard_map/ppermute | solution.py:428
  12.8 5.7 %collective-permute-start.3 = (f32[16,128]{1,0:T(8,128)}, f32[16,128]{1,0:T(8,128)S(1)}, u32[]{:S(2)}, u32[]{:S(2)}) collective-permute-start(f32[16,128]{1,0:T(8,128)} %get-tuple-element.28.refs_4_), channel_id=1, source_target_pairs={{0,3},{1,2},{2,1},{3,0},{4,7},{5,6},{6,5},{7,4},{8,11},{9,10},{10,... | collective-permute-start | bytes 24584 | tf_op jit(solution)/shard_map/ppermute | solution.py:428
  15.1 3.4 %copy-start.14 = (f32[16,128]{1,0:T(8,128)}, f32[16,128]{1,0:T(8,128)S(1)}, u32[]{:S(2)}) copy-start(f32[16,128]{1,0:T(8,128)S(1)} %collective-permute-done.4.refs_7_) | copy-start | bytes 24580
  18.5 0.6 copy-start.17
  18.5 0.7 copy-start.6
  18.5 0.8 copy-start.9
  18.5 0.9 copy-start.3
  46.1 9.7 %collective-permute-start.5 = (f32[74,8,128]{2,1,0:T(8,128)}, f32[74,8,128]{2,1,0:T(8,128)S(1)}, u32[]{:S(2)}, u32[]{:S(2)}) collective-permute-start(f32[74,8,128]{2,1,0:T(8,128)} %get-tuple-element.31), channel_id=1, source_target_pairs={{0,1},{1,0},{2,3},{3,2},{4,5},{5,4},{6,7},{7,6},{8,9},{9,8},{10,11... | collective-permute-start | bytes 909320 | tf_op jit(solution)/shard_map/ppermute | solution.py:423
  46.1 9.7 %collective-permute-start.6 = (f32[2,6,6,8,128]{4,3,2,1,0:T(8,128)}, f32[2,6,6,8,128]{4,3,2,1,0:T(8,128)S(1)}, u32[]{:S(2)}, u32[]{:S(2)}) collective-permute-start(f32[2,6,6,8,128]{4,3,2,1,0:T(8,128)} %get-tuple-element.32), channel_id=1, source_target_pairs={{0,4},{4,8},{8,12},{12,16},{16,20},{20,24},{24,28},{28,0},{1,5},{5... | collective-permute-start | bytes 884744 | tf_op jit(solution)/shard_map/ppermute | solution.py:424
  46.1 9.6 %collective-permute-start.7 = (f32[2,6,6,8,128]{4,3,2,1,0:T(8,128)}, f32[2,6,6,8,128]{4,3,2,1,0:T(8,128)S(1)}, u32[]{:S(2)}, u32[]{:S(2)}) collective-permute-start(f32[2,6,6,8,128]{4,3,2,1,0:T(8,128)} %get-tuple-element.33), channel_id=1, source_target_pairs={{4,0},{8,4},{12,8},{16,12},{20,16},{24,20},{28,24},{0,28},{5,1},{9... | collective-permute-start | bytes 884744 | tf_op jit(solution)/shard_map/ppermute | solution.py:425
  48.8 4.9 %collective-permute-start.9 = (f32[16,128]{1,0:T(8,128)}, f32[16,128]{1,0:T(8,128)S(1)}, u32[]{:S(2)}, u32[]{:S(2)}) collective-permute-start(f32[16,128]{1,0:T(8,128)} %get-tuple-element.34.refs_4_), channel_id=1, source_target_pairs={{0,2},{1,3},{2,0},{3,1},{4,6},{5,7},{6,4},{7,5},{8,10},{9,11},{10,... | collective-permute-start | bytes 24584 | tf_op jit(solution)/shard_map/ppermute | solution.py:428
  49.8 6.0 %collective-permute-start.8 = (f32[16,128]{1,0:T(8,128)}, f32[16,128]{1,0:T(8,128)S(1)}, u32[]{:S(2)}, u32[]{:S(2)}) collective-permute-start(f32[16,128]{1,0:T(8,128)} %get-tuple-element.34.refs_4_), channel_id=1, source_target_pairs={{0,3},{1,2},{2,1},{3,0},{4,7},{5,6},{6,5},{7,4},{8,11},{9,10},{10,... | collective-permute-start | bytes 24584 | tf_op jit(solution)/shard_map/ppermute | solution.py:428
  53.6 2.1 %copy-start.12 = (f32[16,128]{1,0:T(8,128)}, f32[16,128]{1,0:T(8,128)S(1)}, u32[]{:S(2)}) copy-start(f32[16,128]{1,0:T(8,128)S(1)} %collective-permute-done.9.refs_7_) | copy-start | bytes 24580
  55.7 0.6 copy-start.15
  55.7 0.7 copy-start.4
  55.7 0.8 copy-start.7
  55.7 0.9 copy-start.1
  83.3 12.2 %collective-permute-start.10 = (f32[74,8,128]{2,1,0:T(8,128)}, f32[74,8,128]{2,1,0:T(8,128)S(1)}, u32[]{:S(2)}, u32[]{:S(2)}) collective-permute-start(f32[74,8,128]{2,1,0:T(8,128)} %get-tuple-element.36), channel_id=1, source_target_pairs={{0,1},{1,0},{2,3},{3,2},{4,5},{5,4},{6,7},{7,6},{8,9},{9,8},{10,11... | collective-permute-start | bytes 909320 | tf_op jit(solution)/shard_map/ppermute | solution.py:423
  85.1 10.4 %collective-permute-start.11 = (f32[2,6,6,8,128]{4,3,2,1,0:T(8,128)}, f32[2,6,6,8,128]{4,3,2,1,0:T(8,128)S(1)}, u32[]{:S(2)}, u32[]{:S(2)}) collective-permute-start(f32[2,6,6,8,128]{4,3,2,1,0:T(8,128)} %get-tuple-element.37), channel_id=1, source_target_pairs={{0,4},{4,8},{8,12},{12,16},{16,20},{20,24},{24,28},{28,0},{1,5},{5... | collective-permute-start | bytes 884744 | tf_op jit(solution)/shard_map/ppermute | solution.py:424
  85.4 10.1 %collective-permute-start.12 = (f32[2,6,6,8,128]{4,3,2,1,0:T(8,128)}, f32[2,6,6,8,128]{4,3,2,1,0:T(8,128)S(1)}, u32[]{:S(2)}, u32[]{:S(2)}) collective-permute-start(f32[2,6,6,8,128]{4,3,2,1,0:T(8,128)} %get-tuple-element.38), channel_id=1, source_target_pairs={{4,0},{8,4},{12,8},{16,12},{20,16},{24,20},{28,24},{0,28},{5,1},{9... | collective-permute-start | bytes 884744 | tf_op jit(solution)/shard_map/ppermute | solution.py:425
  87.7 5.0 %collective-permute-start.14 = (f32[16,128]{1,0:T(8,128)}, f32[16,128]{1,0:T(8,128)S(1)}, u32[]{:S(2)}, u32[]{:S(2)}) collective-permute-start(f32[16,128]{1,0:T(8,128)} %get-tuple-element.39.refs_4_), channel_id=1, source_target_pairs={{0,2},{1,3},{2,0},{3,1},{4,6},{5,7},{6,4},{7,5},{8,10},{9,11},{10,... | collective-permute-start | bytes 24584 | tf_op jit(solution)/shard_map/ppermute | solution.py:428
  89.5 5.7 %collective-permute-start.13 = (f32[16,128]{1,0:T(8,128)}, f32[16,128]{1,0:T(8,128)S(1)}, u32[]{:S(2)}, u32[]{:S(2)}) collective-permute-start(f32[16,128]{1,0:T(8,128)} %get-tuple-element.39.refs_4_), channel_id=1, source_target_pairs={{0,3},{1,2},{2,1},{3,0},{4,7},{5,6},{6,5},{7,4},{8,11},{9,10},{10,... | collective-permute-start | bytes 24584 | tf_op jit(solution)/shard_map/ppermute | solution.py:428
  92.8 2.7 %copy-start.13 = (f32[16,128]{1,0:T(8,128)}, f32[16,128]{1,0:T(8,128)S(1)}, u32[]{:S(2)}) copy-start(f32[16,128]{1,0:T(8,128)S(1)} %collective-permute-done.14.refs_7_) | copy-start | bytes 24580
  95.2 0.6 copy-start.16
  95.5 0.7 copy-start.5
  95.5 0.8 copy-start.8
  95.5 0.9 copy-start.2
  123.1 10.6 %collective-permute-start.15 = (f32[74,8,128]{2,1,0:T(8,128)}, f32[74,8,128]{2,1,0:T(8,128)S(1)}, u32[]{:S(2)}, u32[]{:S(2)}) collective-permute-start(f32[74,8,128]{2,1,0:T(8,128)} %get-tuple-element.41), channel_id=1, source_target_pairs={{0,1},{1,0},{2,3},{3,2},{4,5},{5,4},{6,7},{7,6},{8,9},{9,8},{10,11... | collective-permute-start | bytes 909320 | tf_op jit(solution)/shard_map/ppermute | solution.py:423
  123.1 10.5 %collective-permute-start.16 = (f32[2,6,6,8,128]{4,3,2,1,0:T(8,128)}, f32[2,6,6,8,128]{4,3,2,1,0:T(8,128)S(1)}, u32[]{:S(2)}, u32[]{:S(2)}) collective-permute-start(f32[2,6,6,8,128]{4,3,2,1,0:T(8,128)} %get-tuple-element.42), channel_id=1, source_target_pairs={{0,4},{4,8},{8,12},{12,16},{16,20},{20,24},{24,28},{28,0},{1,5},{5... | collective-permute-start | bytes 884744 | tf_op jit(solution)/shard_map/ppermute | solution.py:424
  123.6 10.1 %collective-permute-start.17 = (f32[2,6,6,8,128]{4,3,2,1,0:T(8,128)}, f32[2,6,6,8,128]{4,3,2,1,0:T(8,128)S(1)}, u32[]{:S(2)}, u32[]{:S(2)}) collective-permute-start(f32[2,6,6,8,128]{4,3,2,1,0:T(8,128)} %get-tuple-element.43), channel_id=1, source_target_pairs={{4,0},{8,4},{12,8},{16,12},{20,16},{24,20},{28,24},{0,28},{5,1},{9... | collective-permute-start | bytes 884744 | tf_op jit(solution)/shard_map/ppermute | solution.py:425
  125.8 5.2 %collective-permute-start.19 = (f32[16,128]{1,0:T(8,128)}, f32[16,128]{1,0:T(8,128)S(1)}, u32[]{:S(2)}, u32[]{:S(2)}) collective-permute-start(f32[16,128]{1,0:T(8,128)} %get-tuple-element.44.refs_4_), channel_id=1, source_target_pairs={{0,2},{1,3},{2,0},{3,1},{4,6},{5,7},{6,4},{7,5},{8,10},{9,11},{10,... | collective-permute-start | bytes 24584 | tf_op jit(solution)/shard_map/ppermute | solution.py:428
  128.0 5.7 %collective-permute-start.18 = (f32[16,128]{1,0:T(8,128)}, f32[16,128]{1,0:T(8,128)S(1)}, u32[]{:S(2)}, u32[]{:S(2)}) collective-permute-start(f32[16,128]{1,0:T(8,128)} %get-tuple-element.44.refs_4_), channel_id=1, source_target_pairs={{0,3},{1,2},{2,1},{3,0},{4,7},{5,6},{6,5},{7,4},{8,11},{9,10},{10,... | collective-permute-start | bytes 24584 | tf_op jit(solution)/shard_map/ppermute | solution.py:428
  131.0 2.7 %copy-start.18 = (f32[16,128]{1,0:T(8,128)}, f32[16,128]{1,0:T(8,128)S(1)}, u32[]{:S(2)}) copy-start(f32[16,128]{1,0:T(8,128)S(1)} %collective-permute-done.19.refs_7_) | copy-start | bytes 24580
  133.6 0.6 copy-start.19
  133.6 0.7 copy-start.10
  133.7 0.8 copy-start.11
  133.7 0.9 copy-start
